TPU v7x, 32 devices: a whole 2x2x4 slice. The times are simulated.
32 devices in a mesh: row: 4 (over y, x), col: 8 (over z, core).
Axes of the slice: x: 2, y: 2, z: 4, core: 2. Of those that a mesh axis runs over, the one named last changes fastest.
Arguments:
- source: float32 [96, 128, 128], P('row', 'col'), may hold values from -24 to 24
- coefficient: float32 [96, 128, 128], P('row', 'col'), may hold values from 0.5 to 8
Outputs:
- relaxed: float32 [96, 128, 128], P('row', 'col')
All inputs are finite; a program needn't handle non-finite values.
Results may differ from a plain program's by a relative error of at most 0.000071.
Values sent between devices are 32-bit elements; how exact they have to be, the bound alone decides.
A program may use at most 64 MiB of HBM per device.

v0:
```python
import jax
import jax.numpy as jnp
from jax import lax
from jax.sharding import PartitionSpec as P

SWEEPS = 4


DAMPING = 0.8
SCREEN_SHIFT = 0.02
HIGHEST = lax.Precision.HIGHEST


def padded(block, sides, width):
    for axis, dim in sides:
        count = lax.axis_size(axis)
        forward = [(i, i + 1) for i in range(count - 1)]
        backward = [(target, source) for source, target in forward]
        low = lax.ppermute(
            lax.slice_in_dim(block, block.shape[dim] - width, None, axis=dim), axis, forward
        )
        high = lax.ppermute(lax.slice_in_dim(block, 0, width, axis=dim), axis, backward)
        block = jnp.concatenate([low, block, high], axis=dim)
    return block


def sine_table(length):
    series = jnp.arange(length, dtype=jnp.int32) + 1
    phases = series[:, None] * series[None, :] % (2 * (length + 1))
    return jnp.sin(jnp.pi * phases.astype(jnp.float32) / (length + 1))


def eigenvalues(positions, length):
    angles = jnp.pi * (positions + 1).astype(jnp.float32) / (2 * (length + 1))
    return 4.0 * jnp.sin(angles) ** 2


def neighbour_image(wide_field, diagonal_total):
    zpadded = jnp.pad(wide_field, ((0, 0), (0, 0), (1, 1)))
    center = wide_field[1:-1, 1:-1, :]
    beside = (
        wide_field[2:, 1:-1] + wide_field[:-2, 1:-1] + wide_field[1:-1, 2:] + wide_field[1:-1, :-2]
    )
    beside = beside + zpadded[1:-1, 1:-1, 2:] + zpadded[1:-1, 1:-1, :-2]
    return (center, diagonal_total * center - beside)


def relax_once(wide_field, diagonal_total, source):
    center, applied = neighbour_image(wide_field, diagonal_total)
    return center + DAMPING * (source - applied) / diagonal_total


def trim_rim(tensor, margin):
    return tensor[margin : tensor.shape[0] - margin, margin : tensor.shape[1] - margin]


def inside_table(row_cells, col_cells, margin):
    row_ids = (
        lax.axis_index("row") * row_cells
        - margin
        + jnp.arange(row_cells + 2 * margin, dtype=jnp.int32)
    )
    col_ids = (
        lax.axis_index("col") * col_cells
        - margin
        + jnp.arange(col_cells + 2 * margin, dtype=jnp.int32)
    )
    row_inside = (row_ids >= 0) & (row_ids < row_cells * lax.axis_size("row"))
    col_inside = (col_ids >= 0) & (col_ids < col_cells * lax.axis_size("col"))
    return (row_inside[:, None] & col_inside[None, :]).astype(jnp.float32)[:, :, None]


def coarse_solve(residual):
    row_cells, col_cells, z_cells = residual.shape
    coarse_rows = row_cells // 2
    coarse_cols = col_cells // 2
    coarse_z = z_cells // 2
    total_r = coarse_rows * lax.axis_size("row")
    total_c = coarse_cols * lax.axis_size("col")
    z_slab = coarse_z // lax.axis_size("row")
    r_slab = total_r // lax.axis_size("col")
    coarse = residual.reshape(coarse_rows, 2, coarse_cols, 2, coarse_z, 2).sum(axis=(1, 3, 5)) * 0.5
    table_z = sine_table(coarse_z)
    table_r = sine_table(total_r)
    table_c = sine_table(total_c)
    ordered = jnp.transpose(coarse, (2, 1, 0))
    along_z = jnp.dot(table_z, ordered.reshape(coarse_z, -1), precision=HIGHEST).reshape(
        coarse_z, coarse_cols, coarse_rows
    )
    row_lines = lax.all_to_all(along_z, "row", split_axis=0, concat_axis=2, tiled=True)
    along_r = jnp.einsum("zcr,kr->zkc", row_lines, table_r, precision=HIGHEST)
    col_lines = lax.all_to_all(along_r, "col", split_axis=1, concat_axis=2, tiled=True)
    spectrum = jnp.dot(col_lines.reshape(-1, total_c), table_c, precision=HIGHEST).reshape(
        z_slab, r_slab, total_c
    )
    normaliser = (coarse_z + 1.0) * (total_r + 1.0) * (total_c + 1.0) / 8.0
    lam_z = eigenvalues(
        lax.axis_index("row") * z_slab + jnp.arange(z_slab, dtype=jnp.int32), coarse_z
    )
    lam_r = eigenvalues(
        lax.axis_index("col") * r_slab + jnp.arange(r_slab, dtype=jnp.int32), total_r
    )
    lam_c = eigenvalues(jnp.arange(total_c, dtype=jnp.int32), total_c)
    denominator = (
        SCREEN_SHIFT + lam_z[:, None, None] + lam_r[None, :, None] + lam_c[None, None, :]
    ) * normaliser
    scaled = spectrum / denominator
    back_c = jnp.dot(scaled.reshape(-1, total_c), table_c, precision=HIGHEST).reshape(
        z_slab, r_slab, total_c
    )
    returned = lax.all_to_all(back_c, "col", split_axis=2, concat_axis=1, tiled=True)
    back_r = jnp.einsum("zkc,kr->zcr", returned, table_r, precision=HIGHEST)
    owned = lax.all_to_all(back_r, "row", split_axis=2, concat_axis=0, tiled=True)
    back_z = jnp.dot(table_z, owned.reshape(coarse_z, -1), precision=HIGHEST).reshape(
        coarse_z, coarse_cols, coarse_rows
    )
    correction = jnp.transpose(back_z, (2, 1, 0))
    return jnp.broadcast_to(
        correction[:, None, :, None, :, None], (coarse_rows, 2, coarse_cols, 2, coarse_z, 2)
    ).reshape(row_cells, col_cells, z_cells)


def local(source, coefficient):
    row_cells, col_cells, z_cells = source.shape
    diagonal_total = 6.0 + coefficient
    opening = DAMPING * source / diagonal_total
    wide_first, wide_source, wide_coef = (
        padded(opening, (("row", 0), ("col", 1)), SWEEPS),
        padded(source, (("row", 0), ("col", 1)), SWEEPS),
        padded(coefficient, (("row", 0), ("col", 1)), SWEEPS),
    )
    wide_diag = 6.0 + wide_coef
    inside = inside_table(row_cells, col_cells, SWEEPS)
    wide_iter = wide_first
    for repeat in range(1, SWEEPS):
        wide_iter = relax_once(
            wide_iter, trim_rim(wide_diag, repeat), trim_rim(wide_source, repeat)
        ) * trim_rim(inside, repeat)
    iterate, applied = neighbour_image(wide_iter, diagonal_total)
    residual = source - applied
    iterate = iterate + coarse_solve(residual)
    wide_iter = padded(iterate, (("row", 0), ("col", 1)), SWEEPS)
    for repeat in range(1, SWEEPS + 1):
        wide_iter = relax_once(
            wide_iter, trim_rim(wide_diag, repeat), trim_rim(wide_source, repeat)
        ) * trim_rim(inside, repeat)
    return wide_iter


def solution(mesh):
    return jax.shard_map(
        local,
        mesh=mesh,
        in_specs=(P("row", "col", None), P("row", "col", None)),
        out_specs=P("row", "col", None),
        check_vma=False,
    )
```

profile of v0, /device:TPU:3, one launch (start us, length us, event | category | flops | bytes accessed | tf_op | source)
XLA Modules:
  0.0 140.1 jit_solution(14815841773290584275)
XLA Ops:
  0.0 0.8 fusion.138
  0.8 3.1 %collective-permute-start.4 = (f32[4,16,128]{2,1,0:T(8,128)S(1)}, f32[4,16,128]{2,1,0:T(8,128)S(1)}, u32[]{:S(2)}, u32[]{:S(2)}) collective-permute-start(f32[4,16,128]{2,1,0:T(8,128)S(1)} %get-tuple-element.16), channel_id=1, source_target_pairs={{0,8},{8,16},{16,24},{1,9},{9,17},{17,25},{2,10},{10,18},{18,26},{... | collective-permute-start | bytes 98312 | tf_op jit(solution)/shard_map/ppermute | solution.py:19
  4.0 0.8 fusion.139
  4.7 3.1 %collective-permute-start.8 = (f32[4,16,128]{2,1,0:T(8,128)S(1)}, f32[4,16,128]{2,1,0:T(8,128)S(1)}, u32[]{:S(2)}, u32[]{:S(2)}) collective-permute-start(f32[4,16,128]{2,1,0:T(8,128)S(1)} %get-tuple-element.21), channel_id=1, source_target_pairs={{0,8},{8,16},{16,24},{1,9},{9,17},{17,25},{2,10},{10,18},{18,26},{... | collective-permute-start | bytes 98312 | tf_op jit(solution)/shard_map/ppermute | solution.py:19
  7.9 2.2 %collective-permute-start.9 = (f32[4,16,128]{2,1,0:T(8,128)S(1)}, f32[4,16,128]{2,1,0:T(8,128)S(1)}, u32[]{:S(2)}, u32[]{:S(2)}) collective-permute-start(f32[4,16,128]{2,1,0:T(8,128)S(1)} %get-tuple-element.20), channel_id=1, source_target_pairs={{8,0},{16,8},{24,16},{9,1},{17,9},{25,17},{10,2},{18,10},{26,18},{... | collective-permute-start | bytes 98312 | tf_op jit(solution)/shard_map/ppermute | solution.py:22
  10.0 1.9 %collective-permute-start.5 = (f32[4,16,128]{2,1,0:T(8,128)S(1)}, f32[4,16,128]{2,1,0:T(8,128)S(1)}, u32[]{:S(2)}, u32[]{:S(2)}) collective-permute-start(f32[4,16,128]{2,1,0:T(8,128)S(1)} %get-tuple-element.15), channel_id=1, source_target_pairs={{8,0},{16,8},{24,16},{9,1},{17,9},{25,17},{10,2},{18,10},{26,18},{... | collective-permute-start | bytes 98312 | tf_op jit(solution)/shard_map/ppermute | solution.py:22
  12.5 1.1 constant_dynamic-update-slice_fusion.1
  13.6 4.3 %collective-permute-start = (f32[4,16,128]{2,1,0:T(8,128)S(1)}, f32[4,16,128]{2,1,0:T(8,128)S(1)}, u32[]{:S(2)}, u32[]{:S(2)}) collective-permute-start(f32[4,16,128]{2,1,0:T(8,128)S(1)} %get-tuple-element.22), channel_id=1, source_target_pairs={{0,8},{8,16},{16,24},{1,9},{9,17},{17,25},{2,10},{10,18},{18,26},{... | collective-permute-start | bytes 98312 | tf_op jit(solution)/shard_map/ppermute | solution.py:19
  17.9 1.9 %collective-permute-start.1 = (f32[4,16,128]{2,1,0:T(8,128)S(1)}, f32[4,16,128]{2,1,0:T(8,128)S(1)}, u32[]{:S(2)}, u32[]{:S(2)}) collective-permute-start(f32[4,16,128]{2,1,0:T(8,128)S(1)} %get-tuple-element.23), channel_id=1, source_target_pairs={{8,0},{16,8},{24,16},{9,1},{17,9},{25,17},{10,2},{18,10},{26,18},{... | collective-permute-start | bytes 98312 | tf_op jit(solution)/shard_map/ppermute | solution.py:22
  19.8 5.2 %collective-permute-start.10 = (f32[32,4,128]{2,1,0:T(4,128)S(1)}, f32[32,4,128]{2,1,0:T(4,128)S(1)}, u32[]{:S(2)}, u32[]{:S(2)}) collective-permute-start(f32[32,4,128]{2,1,0:T(4,128)S(1)} %get-tuple-element.9), channel_id=1, source_target_pairs={{0,1},{1,2},{2,3},{3,4},{4,5},{5,6},{6,7},{8,9},{9,10},{10,11},{11... | collective-permute-start | bytes 196616 | tf_op jit(solution)/shard_map/ppermute | solution.py:19
  25.0 1.9 %collective-permute-start.11 = (f32[32,4,128]{2,1,0:T(4,128)S(1)}, f32[32,4,128]{2,1,0:T(4,128)S(1)}, u32[]{:S(2)}, u32[]{:S(2)}) collective-permute-start(f32[32,4,128]{2,1,0:T(4,128)S(1)} %get-tuple-element.10), channel_id=1, source_target_pairs={{1,0},{2,1},{3,2},{4,3},{5,4},{6,5},{7,6},{9,8},{10,9},{11,10},{12... | collective-permute-start | bytes 196616 | tf_op jit(solution)/shard_map/ppermute | solution.py:22
  27.0 3.6 %collective-permute-start.6 = (f32[32,4,128]{2,1,0:T(4,128)S(1)}, f32[32,4,128]{2,1,0:T(4,128)S(1)}, u32[]{:S(2)}, u32[]{:S(2)}) collective-permute-start(f32[32,4,128]{2,1,0:T(4,128)S(1)} %get-tuple-element.7), channel_id=1, source_target_pairs={{0,1},{1,2},{2,3},{3,4},{4,5},{5,6},{6,7},{8,9},{9,10},{10,11},{11... | collective-permute-start | bytes 196616 | tf_op jit(solution)/shard_map/ppermute | solution.py:19
  30.7 1.9 %collective-permute-start.7 = (f32[32,4,128]{2,1,0:T(4,128)S(1)}, f32[32,4,128]{2,1,0:T(4,128)S(1)}, u32[]{:S(2)}, u32[]{:S(2)}) collective-permute-start(f32[32,4,128]{2,1,0:T(4,128)S(1)} %get-tuple-element.8), channel_id=1, source_target_pairs={{1,0},{2,1},{3,2},{4,3},{5,4},{6,5},{7,6},{9,8},{10,9},{11,10},{12... | collective-permute-start | bytes 196616 | tf_op jit(solution)/shard_map/ppermute | solution.py:22
  32.6 3.6 %collective-permute-start.2 = (f32[32,4,128]{2,1,0:T(4,128)S(1)}, f32[32,4,128]{2,1,0:T(4,128)S(1)}, u32[]{:S(2)}, u32[]{:S(2)}) collective-permute-start(f32[32,4,128]{2,1,0:T(4,128)S(1)} %get-tuple-element.11), channel_id=1, source_target_pairs={{0,1},{1,2},{2,3},{3,4},{4,5},{5,6},{6,7},{8,9},{9,10},{10,11},{11... | collective-permute-start | bytes 196616 | tf_op jit(solution)/shard_map/ppermute | solution.py:19
  36.3 1.9 %collective-permute-start.3 = (f32[32,4,128]{2,1,0:T(4,128)S(1)}, f32[32,4,128]{2,1,0:T(4,128)S(1)}, u32[]{:S(2)}, u32[]{:S(2)}) collective-permute-start(f32[32,4,128]{2,1,0:T(4,128)S(1)} %get-tuple-element.12), channel_id=1, source_target_pairs={{1,0},{2,1},{3,2},{4,3},{5,4},{6,5},{7,6},{9,8},{10,9},{11,10},{12... | collective-permute-start | bytes 196616 | tf_op jit(solution)/shard_map/ppermute | solution.py:22
  38.4 3.5 %collective-permute-done.3 = f32[32,4,128]{2,1,0:T(4,128)S(1)} collective-permute-done((f32[32,4,128]{2,1,0:T(4,128)S(1)}, f32[32,4,128]{2,1,0:T(4,128)S(1)}, u32[]{:S(2)}, u32[]{:S(2)}) %collective-permute-start.3) | collective-permute-done | bytes 65568 | tf_op jit(solution)/shard_map/ppermute | solution.py:22
  42.0 0.4 fusion.15
  42.3 0.4 fusion.31
  42.7 0.4 fusion.47
  43.1 0.2 fusion.51
  43.3 13.9 %reshape.166 = f32[12,2,8,2,64,2]{5,4,3,2,1,0:T(8,128)} reshape(f32[24,16,128]{2,1,0:T(8,128)S(1)} %fusion.51) | data formatting | bytes 393216 | tf_op jit(solution)/shard_map/reshape | solution.py:82
  57.2 5.5 %reduce_sum.9 = f32[12,8,64]{2,1,0:T(8,128)S(1)} reduce(f32[12,2,8,2,64,2]{5,4,3,2,1,0:T(8,128)} %reshape.166, f32[]{:T(128)} %constant.33.clone.1), dimensions={1,3,5}, to_apply=%region_0.1 | reduce | flops 43008 | bytes 221188 | tf_op jit(solution)/shard_map/reduce_sum | solution.py:82
  62.8 0.4 fusion.75
  63.2 0.2 copy.18
  63.4 0.8 reshape.172
  64.2 4.2 %all-to-all-start = ((f32[4,1,1536]{2,1,0:T(1,128)}), f32[4,1,1536]{2,1,0:T(1,128)S(1)}, u32[]{:S(2)}, u32[]{:S(2)}) async-start(f32[4,1,1536]{2,1,0:T(1,128)} %reshape.172), calls=%async_computation | async-start | bytes 49152 | tf_op jit(solution)/shard_map/all_to_all | solution.py:90
  68.4 2.9 %all-to-all-done = f32[4,1,1536]{2,1,0:T(1,128)S(1)} async-done(((f32[4,1,1536]{2,1,0:T(1,128)}), f32[4,1,1536]{2,1,0:T(1,128)S(1)}, u32[]{:S(2)}, u32[]{:S(2)}) %all-to-all-start) | async-done | bytes 24608 | tf_op jit(solution)/shard_map/all_to_all | solution.py:90
  71.4 0.5 broadcast.258
  71.9 0.7 reduce
  72.6 0.3 reshape.173
  72.9 0.2 copy.49
  73.1 0.2 all_to_all.51
  73.2 0.4 convolution_bitcast_fusion.1
  73.6 0.1 copy.22
  73.7 0.7 reshape.174
  74.5 4.6 %all-to-all-start.1 = ((f32[8,1,768]{2,1,0:T(1,128)}), f32[8,1,768]{2,1,0:T(1,128)S(1)}, u32[]{:S(2)}, u32[]{:S(2)}) async-start(f32[8,1,768]{2,1,0:T(1,128)} %reshape.174), calls=%async_computation.1 | async-start | bytes 49152 | tf_op jit(solution)/shard_map/all_to_all | solution.py:92
  79.1 4.9 %all-to-all-done.1 = f32[8,1,768]{2,1,0:T(1,128)S(1)} async-done(((f32[8,1,768]{2,1,0:T(1,128)}), f32[8,1,768]{2,1,0:T(1,128)S(1)}, u32[]{:S(2)}, u32[]{:S(2)}) %all-to-all-start.1) | async-done | bytes 24608 | tf_op jit(solution)/shard_map/all_to_all | solution.py:92
  84.0 0.7 reduce.1
  84.9 0.5 convolution_divide_fusion
  85.4 0.4 fusion.72
  85.8 0.1 copy.25
  85.9 0.1 reshape.176
  86.1 8.1 %all_to_all.66 = f32[8,1,768]{2,1,0:T(1,128)S(1)} all-to-all(f32[8,1,768]{2,1,0:T(1,128)S(1)} %reshape.176), channel_id=1, replica_groups=mesh['row'=4,'col'=8] {'col'}, dimensions={0} | all-to-all | bytes 49152 | tf_op jit(solution)/shard_map/all_to_all | solution.py:111
  94.1 0.7 reduce.2
  94.8 0.1 reshape.177
  95.0 0.5 fusion.60
  95.5 0.1 copy.29
  95.8 5.9 %all_to_all.67 = f32[4,1,1536]{2,1,0:T(1,128)S(1)} all-to-all(f32[4,1,1536]{2,1,0:T(1,128)S(1)} %reshape.178), channel_id=1, replica_groups=mesh['row'=4,'col'=8] {'row'}, dimensions={0} | all-to-all | bytes 49152 | tf_op jit(solution)/shard_map/all_to_all | solution.py:113
  101.7 0.7 reduce.3
  102.6 0.1 copy.50
  102.7 0.1 reshape.168
  102.8 0.4 convolution_bitcast_fusion
  103.3 5.1 %broadcast_in_dim.2 = f32[12,2,8,2,64,2]{5,4,3,2,1,0:T(8,128)} broadcast(f32[12,8,64]{2,1,0:T(8,128)S(1)} %copy.32), dimensions={0,2,4} | broadcast | bytes 221184 | tf_op jit(solution)/shard_map/broadcast_in_dim | solution.py:118
  108.4 9.8 %reshape.169 = f32[24,16,128]{2,1,0:T(8,128)S(1)} reshape(f32[12,2,8,2,64,2]{5,4,3,2,1,0:T(8,128)} %broadcast_in_dim.2) | data formatting | bytes 393216 | tf_op jit(solution)/shard_map/reshape | solution.py:120
  118.3 3.1 %collective-permute-start.12 = (f32[4,16,128]{2,1,0:T(8,128)S(1)}, f32[4,16,128]{2,1,0:T(8,128)S(1)}, u32[]{:S(2)}, u32[]{:S(2)}) collective-permute-start(f32[4,16,128]{2,1,0:T(8,128)S(1)} %get-tuple-element.13), channel_id=1, source_target_pairs={{0,8},{8,16},{16,24},{1,9},{9,17},{17,25},{2,10},{10,18},{18,26},{... | collective-permute-start | bytes 98312 | tf_op jit(solution)/shard_map/ppermute | solution.py:19
  121.4 2.2 %collective-permute-start.13 = (f32[4,16,128]{2,1,0:T(8,128)S(1)}, f32[4,16,128]{2,1,0:T(8,128)S(1)}, u32[]{:S(2)}, u32[]{:S(2)}) collective-permute-start(f32[4,16,128]{2,1,0:T(8,128)S(1)} %get-tuple-element.14), channel_id=1, source_target_pairs={{8,0},{16,8},{24,16},{9,1},{17,9},{25,17},{10,2},{18,10},{26,18},{... | collective-permute-start | bytes 98312 | tf_op jit(solution)/shard_map/ppermute | solution.py:22
  123.6 3.4 %collective-permute-done.13 = f32[4,16,128]{2,1,0:T(8,128)S(1)} collective-permute-done((f32[4,16,128]{2,1,0:T(8,128)S(1)}, f32[4,16,128]{2,1,0:T(8,128)S(1)}, u32[]{:S(2)}, u32[]{:S(2)}) %collective-permute-start.13) | collective-permute-done | bytes 32800 | tf_op jit(solution)/shard_map/ppermute | solution.py:22
  127.0 5.5 %collective-permute-start.14 = (f32[32,4,128]{2,1,0:T(4,128)S(1)}, f32[32,4,128]{2,1,0:T(4,128)S(1)}, u32[]{:S(2)}, u32[]{:S(2)}) collective-permute-start(f32[32,4,128]{2,1,0:T(4,128)S(1)} %get-tuple-element.5), channel_id=1, source_target_pairs={{0,1},{1,2},{2,3},{3,4},{4,5},{5,6},{6,7},{8,9},{9,10},{10,11},{11... | collective-permute-start | bytes 196616 | tf_op jit(solution)/shard_map/ppermute | solution.py:19
  132.4 1.9 %collective-permute-start.15 = (f32[32,4,128]{2,1,0:T(4,128)S(1)}, f32[32,4,128]{2,1,0:T(4,128)S(1)}, u32[]{:S(2)}, u32[]{:S(2)}) collective-permute-start(f32[32,4,128]{2,1,0:T(4,128)S(1)} %get-tuple-element.6), channel_id=1, source_target_pairs={{1,0},{2,1},{3,2},{4,3},{5,4},{6,5},{7,6},{9,8},{10,9},{11,10},{12... | collective-permute-start | bytes 196616 | tf_op jit(solution)/shard_map/ppermute | solution.py:22
  134.4 3.6 %collective-permute-done.15 = f32[32,4,128]{2,1,0:T(4,128)S(1)} collective-permute-done((f32[32,4,128]{2,1,0:T(4,128)S(1)}, f32[32,4,128]{2,1,0:T(4,128)S(1)}, u32[]{:S(2)}, u32[]{:S(2)}) %collective-permute-start.15) | collective-permute-done | bytes 65568 | tf_op jit(solution)/shard_map/ppermute | solution.py:22
  138.1 0.4 fusion.14
  138.5 0.4 fusion.30
  138.8 0.4 fusion.46
  139.2 0.9 fusion.63
  (55 shorter events, 1.5 us)
Async XLA Ops:
  0.0 43.1 %copy-start = (f32[24,16,128]{2,1,0:T(8,128)S(1)}, f32[24,16,128]{2,1,0:T(8,128)}, u32[]{:S(2)}) copy-start(f32[24,16,128]{2,1,0:T(8,128)} %param.2) | copy-start | bytes 589828
  0.0 43.1 %copy-start.1 = (f32[24,16,128]{2,1,0:T(8,128)S(1)}, f32[24,16,128]{2,1,0:T(8,128)}, u32[]{:S(2)}) copy-start(f32[24,16,128]{2,1,0:T(8,128)} %param.3) | copy-start | bytes 589828
  0.8 11.6 %collective-permute-start.4 = (f32[4,16,128]{2,1,0:T(8,128)S(1)}, f32[4,16,128]{2,1,0:T(8,128)S(1)}, u32[]{:S(2)}, u32[]{:S(2)}) collective-permute-start(f32[4,16,128]{2,1,0:T(8,128)S(1)} %get-tuple-element.16), channel_id=1, source_target_pairs={{0,8},{8,16},{16,24},{1,9},{9,17},{17,25},{2,10},{10,18},{18,26},{... | collective-permute-start | bytes 98312 | tf_op jit(solution)/shard_map/ppermute | solution.py:19
  4.7 7.7 %collective-permute-start.8 = (f32[4,16,128]{2,1,0:T(8,128)S(1)}, f32[4,16,128]{2,1,0:T(8,128)S(1)}, u32[]{:S(2)}, u32[]{:S(2)}) collective-permute-start(f32[4,16,128]{2,1,0:T(8,128)S(1)} %get-tuple-element.21), channel_id=1, source_target_pairs={{0,8},{8,16},{16,24},{1,9},{9,17},{17,25},{2,10},{10,18},{18,26},{... | collective-permute-start | bytes 98312 | tf_op jit(solution)/shard_map/ppermute | solution.py:19
  7.9 11.9 %collective-permute-start.9 = (f32[4,16,128]{2,1,0:T(8,128)S(1)}, f32[4,16,128]{2,1,0:T(8,128)S(1)}, u32[]{:S(2)}, u32[]{:S(2)}) collective-permute-start(f32[4,16,128]{2,1,0:T(8,128)S(1)} %get-tuple-element.20), channel_id=1, source_target_pairs={{8,0},{16,8},{24,16},{9,1},{17,9},{25,17},{10,2},{18,10},{26,18},{... | collective-permute-start | bytes 98312 | tf_op jit(solution)/shard_map/ppermute | solution.py:22
  10.0 16.9 %collective-permute-start.5 = (f32[4,16,128]{2,1,0:T(8,128)S(1)}, f32[4,16,128]{2,1,0:T(8,128)S(1)}, u32[]{:S(2)}, u32[]{:S(2)}) collective-permute-start(f32[4,16,128]{2,1,0:T(8,128)S(1)} %get-tuple-element.15), channel_id=1, source_target_pairs={{8,0},{16,8},{24,16},{9,1},{17,9},{25,17},{10,2},{18,10},{26,18},{... | collective-permute-start | bytes 98312 | tf_op jit(solution)/shard_map/ppermute | solution.py:22
  13.6 17.1 %collective-permute-start = (f32[4,16,128]{2,1,0:T(8,128)S(1)}, f32[4,16,128]{2,1,0:T(8,128)S(1)}, u32[]{:S(2)}, u32[]{:S(2)}) collective-permute-start(f32[4,16,128]{2,1,0:T(8,128)S(1)} %get-tuple-element.22), channel_id=1, source_target_pairs={{0,8},{8,16},{16,24},{1,9},{9,17},{17,25},{2,10},{10,18},{18,26},{... | collective-permute-start | bytes 98312 | tf_op jit(solution)/shard_map/ppermute | solution.py:19
  17.9 14.7 %collective-permute-start.1 = (f32[4,16,128]{2,1,0:T(8,128)S(1)}, f32[4,16,128]{2,1,0:T(8,128)S(1)}, u32[]{:S(2)}, u32[]{:S(2)}) collective-permute-start(f32[4,16,128]{2,1,0:T(8,128)S(1)} %get-tuple-element.23), channel_id=1, source_target_pairs={{8,0},{16,8},{24,16},{9,1},{17,9},{25,17},{10,2},{18,10},{26,18},{... | collective-permute-start | bytes 98312 | tf_op jit(solution)/shard_map/ppermute | solution.py:22
  19.8 16.4 %collective-permute-start.10 = (f32[32,4,128]{2,1,0:T(4,128)S(1)}, f32[32,4,128]{2,1,0:T(4,128)S(1)}, u32[]{:S(2)}, u32[]{:S(2)}) collective-permute-start(f32[32,4,128]{2,1,0:T(4,128)S(1)} %get-tuple-element.9), channel_id=1, source_target_pairs={{0,1},{1,2},{2,3},{3,4},{4,5},{5,6},{6,7},{8,9},{9,10},{10,11},{11... | collective-permute-start | bytes 196616 | tf_op jit(solution)/shard_map/ppermute | solution.py:19
  25.0 13.2 %collective-permute-start.11 = (f32[32,4,128]{2,1,0:T(4,128)S(1)}, f32[32,4,128]{2,1,0:T(4,128)S(1)}, u32[]{:S(2)}, u32[]{:S(2)}) collective-permute-start(f32[32,4,128]{2,1,0:T(4,128)S(1)} %get-tuple-element.10), channel_id=1, source_target_pairs={{1,0},{2,1},{3,2},{4,3},{5,4},{6,5},{7,6},{9,8},{10,9},{11,10},{12... | collective-permute-start | bytes 196616 | tf_op jit(solution)/shard_map/ppermute | solution.py:22
  27.0 11.3 %collective-permute-start.6 = (f32[32,4,128]{2,1,0:T(4,128)S(1)}, f32[32,4,128]{2,1,0:T(4,128)S(1)}, u32[]{:S(2)}, u32[]{:S(2)}) collective-permute-start(f32[32,4,128]{2,1,0:T(4,128)S(1)} %get-tuple-element.7), channel_id=1, source_target_pairs={{0,1},{1,2},{2,3},{3,4},{4,5},{5,6},{6,7},{8,9},{9,10},{10,11},{11... | collective-permute-start | bytes 196616 | tf_op jit(solution)/shard_map/ppermute | solution.py:19
  30.7 7.7 %collective-permute-start.7 = (f32[32,4,128]{2,1,0:T(4,128)S(1)}, f32[32,4,128]{2,1,0:T(4,128)S(1)}, u32[]{:S(2)}, u32[]{:S(2)}) collective-permute-start(f32[32,4,128]{2,1,0:T(4,128)S(1)} %get-tuple-element.8), channel_id=1, source_target_pairs={{1,0},{2,1},{3,2},{4,3},{5,4},{6,5},{7,6},{9,8},{10,9},{11,10},{12... | collective-permute-start | bytes 196616 | tf_op jit(solution)/shard_map/ppermute | solution.py:22
  32.6 5.8 %collective-permute-start.2 = (f32[32,4,128]{2,1,0:T(4,128)S(1)}, f32[32,4,128]{2,1,0:T(4,128)S(1)}, u32[]{:S(2)}, u32[]{:S(2)}) collective-permute-start(f32[32,4,128]{2,1,0:T(4,128)S(1)} %get-tuple-element.11), channel_id=1, source_target_pairs={{0,1},{1,2},{2,3},{3,4},{4,5},{5,6},{6,7},{8,9},{9,10},{10,11},{11... | collective-permute-start | bytes 196616 | tf_op jit(solution)/shard_map/ppermute | solution.py:19
  36.3 5.6 %collective-permute-start.3 = (f32[32,4,128]{2,1,0:T(4,128)S(1)}, f32[32,4,128]{2,1,0:T(4,128)S(1)}, u32[]{:S(2)}, u32[]{:S(2)}) collective-permute-start(f32[32,4,128]{2,1,0:T(4,128)S(1)} %get-tuple-element.12), channel_id=1, source_target_pairs={{1,0},{2,1},{3,2},{4,3},{5,4},{6,5},{7,6},{9,8},{10,9},{11,10},{12... | collective-permute-start | bytes 196616 | tf_op jit(solution)/shard_map/ppermute | solution.py:22
  64.2 7.2 %all-to-all-start = ((f32[4,1,1536]{2,1,0:T(1,128)}), f32[4,1,1536]{2,1,0:T(1,128)S(1)}, u32[]{:S(2)}, u32[]{:S(2)}) async-start(f32[4,1,1536]{2,1,0:T(1,128)} %reshape.172), calls=%async_computation | async-start | bytes 49152 | tf_op jit(solution)/shard_map/all_to_all | solution.py:90
  74.5 9.6 %all-to-all-start.1 = ((f32[8,1,768]{2,1,0:T(1,128)}), f32[8,1,768]{2,1,0:T(1,128)S(1)}, u32[]{:S(2)}, u32[]{:S(2)}) async-start(f32[8,1,768]{2,1,0:T(1,128)} %reshape.174), calls=%async_computation.1 | async-start | bytes 49152 | tf_op jit(solution)/shard_map/all_to_all | solution.py:92
  118.3 5.3 %collective-permute-start.12 = (f32[4,16,128]{2,1,0:T(8,128)S(1)}, f32[4,16,128]{2,1,0:T(8,128)S(1)}, u32[]{:S(2)}, u32[]{:S(2)}) collective-permute-start(f32[4,16,128]{2,1,0:T(8,128)S(1)} %get-tuple-element.13), channel_id=1, source_target_pairs={{0,8},{8,16},{16,24},{1,9},{9,17},{17,25},{2,10},{10,18},{18,26},{... | collective-permute-start | bytes 98312 | tf_op jit(solution)/shard_map/ppermute | solution.py:19
  121.4 5.6 %collective-permute-start.13 = (f32[4,16,128]{2,1,0:T(8,128)S(1)}, f32[4,16,128]{2,1,0:T(8,128)S(1)}, u32[]{:S(2)}, u32[]{:S(2)}) collective-permute-start(f32[4,16,128]{2,1,0:T(8,128)S(1)} %get-tuple-element.14), channel_id=1, source_target_pairs={{8,0},{16,8},{24,16},{9,1},{17,9},{25,17},{10,2},{18,10},{26,18},{... | collective-permute-start | bytes 98312 | tf_op jit(solution)/shard_map/ppermute | solution.py:22
  127.0 7.5 %collective-permute-start.14 = (f32[32,4,128]{2,1,0:T(4,128)S(1)}, f32[32,4,128]{2,1,0:T(4,128)S(1)}, u32[]{:S(2)}, u32[]{:S(2)}) collective-permute-start(f32[32,4,128]{2,1,0:T(4,128)S(1)} %get-tuple-element.5), channel_id=1, source_target_pairs={{0,1},{1,2},{2,3},{3,4},{4,5},{5,6},{6,7},{8,9},{9,10},{10,11},{11... | collective-permute-start | bytes 196616 | tf_op jit(solution)/shard_map/ppermute | solution.py:19
  132.4 5.6 %collective-permute-start.15 = (f32[32,4,128]{2,1,0:T(4,128)S(1)}, f32[32,4,128]{2,1,0:T(4,128)S(1)}, u32[]{:S(2)}, u32[]{:S(2)}) collective-permute-start(f32[32,4,128]{2,1,0:T(4,128)S(1)} %get-tuple-element.6), channel_id=1, source_target_pairs={{1,0},{2,1},{3,2},{4,3},{5,4},{6,5},{7,6},{9,8},{10,9},{11,10},{12... | collective-permute-start | bytes 196616 | tf_op jit(solution)/shard_map/ppermute | solution.py:22
where the time goes:
time: 141 us; the launch traced here: 140 us
  starting transfers between devices  56.2 us (40%)
  local copies, waits for them, and re-layouts  35.1 us (25%)
  waiting for transfers between devices  18.3 us (13%)
  blocking collectives  14 us (10%)
  other arithmetic  13.3 us (9%)
  matrix products  2.59 us (2%)
    ppermute x8, starting transfers between devices, padded(): lax.ppermute(lax.slice_in_dim(block, block.shape[dim] - width, None, axis...  31.5 us
    ppermute x8, starting transfers between devices, padded(): lax.ppermute(lax.slice_in_dim(block, 0, width, axis=dim), axis, backward)  15.9 us
    reshape x1, local copies, waits for them, and re-layouts, coarse_solve(): residual.reshape(coarse_rows, 2, coarse_cols, 2, coarse_z, 2)  13.9 us
    ppermute x8, waiting for transfers between devices, padded(): lax.ppermute(lax.slice_in_dim(block, 0, width, axis=dim), axis, backward)  10.4 us
    reshape x1, local copies, waits for them, and re-layouts, coarse_solve(): return jnp.broadcast_to(correction[:, None, :, None, :, None], (coarse_ro...  9.77 us
    all_to_all x1, blocking collectives, coarse_solve(): lax.all_to_all(back_c, 'col', split_axis=2, concat_axis=1, tiled=True)  8.07 us
    all_to_all x1, blocking collectives, coarse_solve(): lax.all_to_all(back_r, 'row', split_axis=2, concat_axis=0, tiled=True)  5.94 us
    reduce_sum x1, other arithmetic, coarse_solve(): residual.reshape(coarse_rows, 2, coarse_cols, 2, coarse_z, 2)  5.5 us
  transfers between devices with their start and end apart: 18, of which 5 were waited for; matrix products, arithmetic and copies ran while one was open for 2% of the time, Pallas kernels for 0%

commit v1 on v0

--- a/solution.py
+++ b/solution.py
@@ -1,6 +1,9 @@
 import jax
 import jax.numpy as jnp
+import numpy as np
 from jax import lax
+from jax.experimental import pallas as pl
+from jax.experimental.pallas import tpu as pltpu
 from jax.sharding import PartitionSpec as P
 
 SWEEPS = 4
@@ -120,7 +123,7 @@
     ).reshape(row_cells, col_cells, z_cells)
 
 
-def local(source, coefficient):
+def local_general(source, coefficient):
     row_cells, col_cells, z_cells = source.shape
     diagonal_total = 6.0 + coefficient
     opening = DAMPING * source / diagonal_total
@@ -147,7 +150,441 @@
     return wide_iter
 
 
+MESH = pl.DeviceIdType.MESH
+SUBLANES = 8
+
+
+def plain_sine(length):
+    series = np.arange(length) + 1
+    phases = series[:, None] * series[None, :] % (2 * (length + 1))
+    return np.sin(np.pi * phases / (length + 1))
+
+
+def plain_eigen(length):
+    return 4.0 * np.sin(np.pi * (np.arange(length) + 1) / (2 * (length + 1))) ** 2
+
+
+def solve_tables(n_row, n_col, kept, coarse_rows, coarse_cols, coarse_z):
+    blocks = n_col * kept
+    total_r, total_c = n_row * coarse_rows, n_col * coarse_cols
+    sine_z, sine_r, sine_c = plain_sine(coarse_z), plain_sine(total_r), plain_sine(total_c)
+    table_z = np.repeat(sine_z, 2, axis=1)
+    forward_r = np.zeros((total_r, n_row, blocks))
+    forward_r[:, :, :coarse_rows] = sine_r.reshape(total_r, n_row, coarse_rows)
+    window_r = np.zeros((n_row, blocks, total_r))
+    margin = (blocks - coarse_rows) // 2
+    for r in range(n_row):
+        for a in range(blocks):
+            at = coarse_rows * r - margin + a
+            if 0 <= at < total_r:
+                window_r[r, a] = sine_r[at]
+    table_c = np.zeros((n_col, kept, coarse_cols, kept, total_c))
+    for k in range(kept):
+        table_c[:, k, :, k, :] = sine_c.reshape(n_col, coarse_cols, total_c)
+    normaliser = (coarse_z + 1.0) * (total_r + 1.0) * (total_c + 1.0) / 8.0
+    base = SCREEN_SHIFT + plain_eigen(total_r)[:, None] + np.tile(plain_eigen(total_c), kept)[None, :]
+    lam_z = np.repeat(plain_eigen(coarse_z).reshape(n_row * n_col, 1, kept), total_c, axis=2)
+    lanes = kept * total_c
+    tables = (
+        table_z,
+        forward_r.reshape(total_r, n_row * blocks),
+        window_r.reshape(n_row * blocks, total_r),
+        table_c.reshape(lanes, lanes),
+        base * 2.0 * normaliser,
+        lam_z * 2.0 * normaliser,
+    )
+    return tuple(np.asarray(t, np.float32) for t in tables)
+
+
+def block_transpose(x, width):
+    rows, lanes = x.shape
+    row = lax.broadcasted_iota(jnp.int32, x.shape, 0)
+    group = lax.broadcasted_iota(jnp.int32, x.shape, 1) // width
+    step = 1
+    while step < rows:
+        row_bit = (row & step) != 0
+        group_bit = (group & step) != 0
+        from_below = pltpu.roll(pltpu.roll(x, width * step, 1), rows - step, 0)
+        from_above = pltpu.roll(pltpu.roll(x, lanes - width * step, 1), step, 0)
+        x = jnp.where(row_bit == group_bit, x, jnp.where(group_bit, from_below, from_above))
+        step *= 2
+    return x
+
+
+def exact_dot(a, b, contract):
+    return lax.dot_general(
+        a, b, (contract, ((), ())), precision=HIGHEST, preferred_element_type=jnp.float32
+    )
+
+
+def step_kernel(
+    sizes,
+    source,
+    coefficient,
+    table_z,
+    forward_r,
+    window_r,
+    table_c,
+    base,
+    lam_z,
+    out,
+    wide_s,
+    wide_c,
+    weight,
+    first,
+    field_a,
+    field_b,
+    rows_sum,
+    fine_corr,
+    send_a,
+    recv_a,
+    send_b,
+    recv_b,
+    own_sem,
+    halo_send,
+    halo_recv,
+    fwd_send,
+    fwd_recv,
+    back_send,
+    back_recv,
+    ready,
+):
+    n_row, n_col, kept = sizes
+    row_cells, col_cells, z_cells = source.shape
+    coarse_rows, coarse_cols = row_cells // 2, col_cells // 2
+    blocks = n_col * kept
+    devices = n_row * n_col
+    halo_r, halo_c = (wide_s.shape[0] - row_cells) // 2, SUBLANES
+    wide_cols = wide_s.shape[1]
+    my_row, my_col = lax.axis_index("row"), lax.axis_index("col")
+    me = my_row * n_col + my_col
+
+    steps = [(dr, dc) for dr in (-1, 0, 1) for dc in (-1, 0, 1) if (dr, dc) != (0, 0)]
+
+    def exists(dr, dc):
+        r, c = my_row + dr, my_col + dc
+        return (r >= 0) & (r < n_row) & (c >= 0) & (c < n_col)
+
+    barrier = pltpu.get_barrier_semaphore()
+    for d in range(1, n_row):
+        pl.semaphore_signal(
+            barrier, 1, device_id=(lax.rem(my_row + d, n_row), my_col), device_id_type=MESH
+        )
+    for d in range(1, n_col):
+        pl.semaphore_signal(
+            barrier, 1, device_id=(my_row, lax.rem(my_col + d, n_col)), device_id_type=MESH
+        )
+    greeted = n_row + n_col - 2
+    for dr, dc in steps:
+        if dr and dc:
+            there = exists(dr, dc)
+
+            @pl.when(there)
+            def _():
+                pl.semaphore_signal(
+                    barrier, 1, device_id=(my_row + dr, my_col + dc), device_id_type=MESH
+                )
+
+            greeted = greeted + there.astype(jnp.int32)
+
+    arrays = ((source, wide_s), (coefficient, wide_c))
+    own = [
+        pltpu.make_async_copy(
+            here, wide.at[pl.ds(halo_r, row_cells), pl.ds(0, col_cells)], own_sem.at[n]
+        )
+        for n, (here, wide) in enumerate(arrays)
+    ]
+    for copy in own:
+        copy.start()
+
+    def landing(dr, dc):
+        rows = {-1: (0, halo_r), 0: (halo_r, row_cells), 1: (halo_r + row_cells, halo_r)}[dr]
+        cols = {
+            -1: (col_cells + halo_c, halo_c),
+            0: (0, col_cells),
+            1: (col_cells, halo_c),
+        }[dc]
+        return pl.ds(*rows), pl.ds(*cols)
+
+    def leaving(dr, dc):
+        rows = {-1: (0, halo_r), 0: (0, row_cells), 1: (row_cells - halo_r, halo_r)}[dr]
+        cols = {-1: (0, halo_c), 0: (0, col_cells), 1: (col_cells - halo_c, halo_c)}[dc]
+        return pl.ds(*rows), pl.ds(*cols)
+
+    def halo_copy(n, at):
+        dr, dc = steps[at]
+        here, wide = arrays[n]
+        return pltpu.make_async_remote_copy(
+            src_ref=here.at[leaving(dr, dc)],
+            dst_ref=wide.at[landing(-dr, -dc)],
+            send_sem=halo_send.at[n, at],
+            recv_sem=halo_recv.at[n, at],
+            device_id=(my_row + dr, my_col + dc),
+            device_id_type=MESH,
+        )
+
+    pl.semaphore_wait(barrier, greeted)
+    for at in range(len(steps)):
+
+        @pl.when(exists(*steps[at]))
+        def _():
+            for n in range(2):
+                halo_copy(n, at).start()
+
+    for d in range(1, n_row):
+        pl.semaphore_signal(
+            ready, 1, device_id=(lax.rem(my_row + d, n_row), my_col), device_id_type=MESH
+        )
+
+    for at, (dr, dc) in enumerate(steps):
+
+        @pl.when(jnp.logical_not(exists(dr, dc)))
+        def _():
+            rows, cols = landing(dr, dc)
+            wide_s[rows, cols] = jnp.zeros((rows.size, cols.size, z_cells), jnp.float32)
+            wide_c[rows, cols] = jnp.zeros((rows.size, cols.size, z_cells), jnp.float32)
+
+    for copy in own:
+        copy.wait()
+    for at in range(len(steps)):
+        @pl.when(exists(*steps[len(steps) - 1 - at]))
+        def _():
+            for n in range(2):
+                halo_copy(n, at).wait_recv()
+
+    wide_rows = wide_s.shape[0]
+    col_at = lax.broadcasted_iota(jnp.int32, (wide_cols, z_cells), 0)
+    z_at = lax.broadcasted_iota(jnp.int32, (wide_cols, z_cells), 1)
+    col_at = my_col * col_cells + jnp.where(col_at >= col_cells + halo_c, col_at - wide_cols, col_at)
+    col_inside = (col_at >= 0) & (col_at < n_col * col_cells)
+    not_first = z_at > 0
+    not_last = z_at < z_cells - 1
+
+    @pl.loop(0, wide_rows)
+    def _(i):
+        at = my_row * row_cells + i - halo_r
+        inside = (at >= 0) & (at < n_row * row_cells)
+        scale = jnp.where(inside & col_inside, DAMPING / (6.0 + wide_c[i]), 0.0)
+        weight[i] = scale
+        start = scale * wide_s[i]
+        first[i] = start
+        field_a[i] = start
+
+    def beside(above, here, below):
+        cols = here.shape[0]
+        low = jnp.where(not_first[:cols], pltpu.roll(here, 1, 1), 0.0)
+        high = jnp.where(not_last[:cols], pltpu.roll(here, z_cells - 1, 1), 0.0)
+        return (
+            (above + below)
+            + (pltpu.roll(here, 1, 0) + pltpu.roll(here, cols - 1, 0))
+            + (low + high)
+        )
+
+    def sweep(old, new, low, high, chunk, shift=0, cols=wide_cols):
+        @pl.loop(0, (high - low) // chunk)
+        def _(n):
+            i = low + n * chunk
+            lines = [old[i - 1 + m] for m in range(chunk + 2)]
+            for m in range(chunk):
+                here = lines[m + 1]
+                fresh = (1.0 - DAMPING) * here + (
+                    first[i + m] + weight[i + m] * beside(lines[m], here, lines[m + 2])
+                )
+                new[i + m - shift] = fresh[:cols]
+
+    fields = (field_a, field_b)
+    for turn in range(1, SWEEPS):
+        sweep(fields[(turn - 1) % 2], fields[turn % 2], 1, wide_rows - 1, 4)
+    smooth, other = fields[(SWEEPS - 1) % 2], fields[SWEEPS % 2]
+
+    @pl.loop(0, coarse_rows)
+    def _(a):
+        i = halo_r + 2 * a
+        lines = [smooth[i - 1 + m] for m in range(4)]
+        total = None
+        for m in range(2):
+            near = beside(lines[m], lines[m + 1], lines[m + 2])
+            left = wide_s[i + m] + (near - (6.0 + wide_c[i + m]) * lines[m + 1])
+            total = left if total is None else total + left
+        rows_sum[a] = total[:col_cells]
+
+    pairs = [
+        rows_sum[a, pl.ds(0, coarse_cols, stride=2), :]
+        + rows_sum[a, pl.ds(1, coarse_cols, stride=2), :]
+        for a in range(coarse_rows)
+    ]
+    blank = jnp.zeros(((blocks - coarse_rows) * coarse_cols, z_cells), jnp.float32)
+    along_z = exact_dot(
+        table_z[...], jnp.concatenate(pairs + [blank], axis=0), ((1,), (1,))
+    )
+    for q in range(devices):
+        send_a[q] = along_z[q * kept : (q + 1) * kept]
+
+    pl.semaphore_wait(ready, n_row - 1)
+
+    def exchange(send, recv, send_sem, recv_sem):
+        def copy(d):
+            target = lax.rem(me + d, devices)
+            return pltpu.make_async_remote_copy(
+                src_ref=send.at[target],
+                dst_ref=recv.at[me],
+                send_sem=send_sem.at[d],
+                recv_sem=recv_sem.at[d],
+                device_id=(lax.div(target, n_col), lax.rem(target, n_col)),
+                device_id_type=MESH,
+            )
+
+        @pl.loop(1, devices)
+        def _(d):
+            copy(d).start()
+
+        recv[me] = send[me]
+
+        @pl.loop(1, devices)
+        def _(d):
+            copy(d).wait_recv()
+
+        return copy
+
+    forward = exchange(send_a, recv_a, fwd_send, fwd_recv)
+
+    gathered = jnp.concatenate(
+        [
+            block_transpose(
+                recv_a[pl.ds(r * n_col, n_col)].reshape(blocks, z_cells), coarse_cols
+            )
+            for r in range(n_row)
+        ],
+        axis=0,
+    )
+    along_r = exact_dot(forward_r[...], gathered, ((1,), (0,)))
+    spectrum = exact_dot(along_r, table_c[...], ((1,), (0,)))
+    scaled = spectrum / (base[...] + lam_z[me])
+    back_c = exact_dot(scaled, table_c[...], ((1,), (1,)))
+    back_r = exact_dot(window_r[...], back_c, ((1,), (0,)))
+    lane = lax.broadcasted_iota(jnp.int32, (blocks, z_cells), 1)
+    column = lane // (kept * coarse_cols)
+    late = lane % coarse_cols >= coarse_cols // 2
+    for r in range(n_row):
+        plane = back_r[r * blocks : (r + 1) * blocks]
+        right = jnp.where(
+            column < n_col - 1, pltpu.roll(plane, z_cells - kept * coarse_cols, 1), 0.0
+        )
+        left = jnp.where(column > 0, pltpu.roll(plane, kept * coarse_cols, 1), 0.0)
+        at = pl.ds(r * n_col, n_col)
+        send_b[at, pl.ds(0, kept)] = block_transpose(plane, coarse_cols).reshape(
+            n_col, kept, z_cells
+        )
+        send_b[at, pl.ds(kept, kept)] = block_transpose(
+            jnp.where(late, left, right), coarse_cols
+        ).reshape(n_col, kept, z_cells)
+
+    backward = exchange(send_b, recv_b, back_send, back_recv)
+
+    modes = devices * kept
+    for part in range(2):
+        lines = recv_b[:, pl.ds(part * kept, kept)].reshape(modes, z_cells)
+        values = exact_dot(jnp.transpose(lines), table_z[...], ((1,), (0,)))
+        for a in range(blocks):
+            for odd in range(2):
+                fine_corr[a, pl.ds(part * col_cells + odd, coarse_cols, stride=2), :] = values[
+                    a * coarse_cols : (a + 1) * coarse_cols
+                ]
+
+    margin = halo_r - (blocks - coarse_rows)
+
+    @pl.loop(0, blocks)
+    def _(a):
+        i = margin + 2 * a
+        smooth[i] = smooth[i] + fine_corr[a]
+        smooth[i + 1] = smooth[i + 1] + fine_corr[a]
+
+    fields = (smooth, other)
+    for turn in range(SWEEPS):
+        low, high = margin + 1 + turn, wide_rows - margin - 1 - turn
+        if turn < SWEEPS - 1:
+            sweep(fields[turn % 2], fields[(turn + 1) % 2], low, high, 2)
+        else:
+            sweep(fields[turn % 2], out, low, high, 2, low, col_cells)
+
+    for at in range(len(steps)):
+
+        @pl.when(exists(*steps[at]))
+        def _():
+            for n in range(2):
+                halo_copy(n, at).wait_send()
+
+    @pl.loop(1, devices)
+    def _(d):
+        forward(d).wait_send()
+        backward(d).wait_send()
+
+
+def local_kernel(n_row, n_col, source, coefficient):
+    row_cells, col_cells, z_cells = source.shape
+    coarse_rows, coarse_cols, coarse_z = row_cells // 2, col_cells // 2, z_cells // 2
+    devices = n_row * n_col
+    kept = coarse_z // devices
+    blocks = n_col * kept
+    tables = solve_tables(n_row, n_col, kept, coarse_rows, coarse_cols, coarse_z)
+    wide = (row_cells + 2 * (2 * SWEEPS - 1), col_cells + 2 * SUBLANES, z_cells)
+    dma = pltpu.SemaphoreType.DMA
+    f32 = jnp.float32
+
+    def body(*refs):
+        step_kernel((n_row, n_col, kept), *refs)
+
+    return pl.pallas_call(
+        body,
+        out_shape=jax.ShapeDtypeStruct(source.shape, f32),
+        in_specs=[pl.BlockSpec(memory_space=pl.ANY)] * 2
+        + [pl.BlockSpec(memory_space=pltpu.VMEM)] * len(tables),
+        out_specs=pl.BlockSpec(memory_space=pltpu.VMEM),
+        scratch_shapes=[pltpu.VMEM(wide, f32)] * 6
+        + [
+            pltpu.VMEM((coarse_rows, col_cells, z_cells), f32),
+            pltpu.VMEM((blocks, 2 * col_cells, z_cells), f32),
+            pltpu.VMEM((devices, kept, z_cells), f32),
+            pltpu.VMEM((devices, kept, z_cells), f32),
+            pltpu.VMEM((devices, 2 * kept, z_cells), f32),
+            pltpu.VMEM((devices, 2 * kept, z_cells), f32),
+            dma((2,)),
+            dma((2, 8)),
+            dma((2, 8)),
+            dma((devices,)),
+            dma((devices,)),
+            dma((devices,)),
+            dma((devices,)),
+            pltpu.SemaphoreType.REGULAR,
+        ],
+        compiler_params=pltpu.CompilerParams(collective_id=0, has_side_effects=True),
+        name="vstep",
+    )(source, coefficient, *(jnp.asarray(t) for t in tables))
+
+
+def fits_kernel(n_row, n_col, source):
+    row_cells, col_cells, z_cells = source.shape
+    devices = n_row * n_col
+    kept = (z_cells // 2) // devices
+    blocks = n_col * kept
+    return (
+        kept * devices * 2 == z_cells
+        and z_cells == 128
+        and col_cells == 2 * SUBLANES
+        and blocks * (col_cells // 2) == z_cells
+        and blocks == row_cells // 2 + SWEEPS
+        and row_cells >= 2 * SWEEPS - 1
+    )
+
+
 def solution(mesh):
+    n_row, n_col = mesh.shape["row"], mesh.shape["col"]
+
+    def local(source, coefficient):
+        if fits_kernel(n_row, n_col, source):
+            return local_kernel(n_row, n_col, source, coefficient)
+        return local_general(source, coefficient)
+
     return jax.shard_map(
         local,
         mesh=mesh,

time: 141 us -> 42.1 us (0.30)
  the two profiles are of different devices: /device:TPU:3 before, /device:TPU:0 now
where the time goes in v1:
time: 42.1 us; the launch traced here: 41.9 us
  Pallas kernels  40.3 us (96%)
  local copies, waits for them, and re-layouts  1.62 us (4%)
    pallas_call x1, Pallas kernels, local_kernel(): pl.pallas_call(body, out_shape=jax.ShapeDtypeStruct(source.shape, f32), i...  40.3 us
    unnamed x1, local copies, waits for them, and re-layouts  1.62 us

profile of v1, /device:TPU:0, one launch (start us, length us, event | category | flops | bytes accessed | tf_op | source)
XLA Modules:
  0.0 41.9 jit_solution(1440331081229126083)
XLA Ops:
  0.0 40.3 %vstep.1 = f32[24,16,128]{2,1,0:T(8,128)} custom-call(f32[24,16,128]{2,1,0:T(8,128)} %refs_0_.1, f32[24,16,128]{2,1,0:T(8,128)} %refs_1_.1, f32[64,128]{1,0:T(8,128)} %constant.12.clone.refs_2_, f32[48,64]{1,0:T(8,128)} %constant.13.clone.refs_3_, f32[64,48]{1,0:T(8,128)} %constant.14.clone.refs_4_, f32[128,128]{1,0:T(8,128)} %constant.15.clone.refs_5_, ...), custom_call_target="tpu_custom_call" | custom-call | tf_op jit(solution)/shard_map/vstep/pallas_call | solution.py:537
  40.3 1.6 %copy.10 = f32[24,16,128]{2,1,0:T(8,128)} copy(f32[24,16,128]{2,1,0:T(8,128)} %vstep.1) | data formatting | bytes 393216

commit v2 on v1

--- a/solution.py
+++ b/solution.py
@@ -152,6 +152,7 @@
 
 MESH = pl.DeviceIdType.MESH
 SUBLANES = 8
+MOST_ROWS = 15
 
 
 def plain_sine(length):
@@ -221,13 +222,19 @@
     sizes,
     source,
     coefficient,
+    table_z_in,
+    forward_r_in,
+    window_r_in,
+    table_c_in,
+    base_in,
+    lam_z_in,
+    out,
     table_z,
     forward_r,
     window_r,
     table_c,
     base,
     lam_z,
-    out,
     wide_s,
     wide_c,
     weight,
@@ -241,6 +248,7 @@
     send_b,
     recv_b,
     own_sem,
+    table_sem,
     halo_send,
     halo_recv,
     fwd_send,
@@ -296,9 +304,35 @@
     ]
     for copy in own:
         copy.start()
-
-    def landing(dr, dc):
-        rows = {-1: (0, halo_r), 0: (halo_r, row_cells), 1: (halo_r + row_cells, halo_r)}[dr]
+    staged = [
+        pltpu.make_async_copy(given, held, table_sem.at[n])
+        for n, (given, held) in enumerate(
+            (
+                (table_z_in, table_z),
+                (forward_r_in, forward_r),
+                (window_r_in, window_r),
+                (table_c_in, table_c),
+                (base_in, base),
+                (lam_z_in, lam_z),
+            )
+        )
+    ]
+    for copy in staged:
+        copy.start()
+
+    near_r = SWEEPS
+    far_r = halo_r - near_r
+    portions = (steps, [step for step in steps if step[0]])
+
+    def landing(far, dr, dc):
+        if far:
+            rows = {-1: (0, far_r), 1: (halo_r + row_cells + near_r, far_r)}[dr]
+        else:
+            rows = {
+                -1: (far_r, near_r),
+                0: (halo_r, row_cells),
+                1: (halo_r + row_cells, near_r),
+            }[dr]
         cols = {
             -1: (col_cells + halo_c, halo_c),
             0: (0, col_cells),
@@ -306,51 +340,64 @@
         }[dc]
         return pl.ds(*rows), pl.ds(*cols)
 
-    def leaving(dr, dc):
-        rows = {-1: (0, halo_r), 0: (0, row_cells), 1: (row_cells - halo_r, halo_r)}[dr]
+    def leaving(far, dr, dc):
+        if far:
+            rows = {-1: (near_r, far_r), 1: (row_cells - halo_r, far_r)}[dr]
+        else:
+            rows = {-1: (0, near_r), 0: (0, row_cells), 1: (row_cells - near_r, near_r)}[dr]
         cols = {-1: (0, halo_c), 0: (0, col_cells), 1: (col_cells - halo_c, halo_c)}[dc]
         return pl.ds(*rows), pl.ds(*cols)
 
-    def halo_copy(n, at):
-        dr, dc = steps[at]
-        here, wide = arrays[n]
-        return pltpu.make_async_remote_copy(
-            src_ref=here.at[leaving(dr, dc)],
-            dst_ref=wide.at[landing(-dr, -dc)],
-            send_sem=halo_send.at[n, at],
-            recv_sem=halo_recv.at[n, at],
-            device_id=(my_row + dr, my_col + dc),
-            device_id_type=MESH,
-        )
+    def halo_copies(far, dr, dc):
+        at = steps.index((dr, dc))
+        return [
+            pltpu.make_async_remote_copy(
+                src_ref=here.at[leaving(far, dr, dc)],
+                dst_ref=wide.at[landing(far, -dr, -dc)],
+                send_sem=halo_send.at[far, n, at],
+                recv_sem=halo_recv.at[far, n, at],
+                device_id=(my_row + dr, my_col + dc),
+                device_id_type=MESH,
+            )
+            for n, (here, wide) in enumerate(arrays)
+        ]
+
+    def start_halo(far):
+        for step in portions[far]:
+
+            @pl.when(exists(*step))
+            def _():
+                for copy in halo_copies(far, *step):
+                    copy.start()
+
+    def fill_halo(far):
+        for step in portions[far]:
+
+            @pl.when(jnp.logical_not(exists(*step)))
+            def _():
+                rows, cols = landing(far, *step)
+                for _, wide in arrays:
+                    wide[rows, cols] = jnp.zeros((rows.size, cols.size, z_cells), jnp.float32)
+
+    def wait_halo(far):
+        for dr, dc in portions[far]:
+            @pl.when(exists(-dr, -dc))
+            def _():
+                for copy in halo_copies(far, dr, dc):
+                    copy.wait_recv()
 
     pl.semaphore_wait(barrier, greeted)
-    for at in range(len(steps)):
-
-        @pl.when(exists(*steps[at]))
-        def _():
-            for n in range(2):
-                halo_copy(n, at).start()
-
+    start_halo(0)
     for d in range(1, n_row):
         pl.semaphore_signal(
             ready, 1, device_id=(lax.rem(my_row + d, n_row), my_col), device_id_type=MESH
         )
-
-    for at, (dr, dc) in enumerate(steps):
-
-        @pl.when(jnp.logical_not(exists(dr, dc)))
-        def _():
-            rows, cols = landing(dr, dc)
-            wide_s[rows, cols] = jnp.zeros((rows.size, cols.size, z_cells), jnp.float32)
-            wide_c[rows, cols] = jnp.zeros((rows.size, cols.size, z_cells), jnp.float32)
-
+    start_halo(1)
+    fill_halo(0)
+    fill_halo(1)
     for copy in own:
         copy.wait()
-    for at in range(len(steps)):
-        @pl.when(exists(*steps[len(steps) - 1 - at]))
-        def _():
-            for n in range(2):
-                halo_copy(n, at).wait_recv()
+    wait_halo(0)
 
     wide_rows = wide_s.shape[0]
     col_at = lax.broadcasted_iota(jnp.int32, (wide_cols, z_cells), 0)
@@ -360,15 +407,19 @@
     not_first = z_at > 0
     not_last = z_at < z_cells - 1
 
-    @pl.loop(0, wide_rows)
-    def _(i):
+    def prepare(i):
         at = my_row * row_cells + i - halo_r
         inside = (at >= 0) & (at < n_row * row_cells)
         scale = jnp.where(inside & col_inside, DAMPING / (6.0 + wide_c[i]), 0.0)
         weight[i] = scale
-        start = scale * wide_s[i]
-        first[i] = start
-        field_a[i] = start
+        first[i] = scale * wide_s[i]
+
+    piece = SUBLANES // 2
+
+    @pl.loop(0, (row_cells + 2 * near_r) // piece)
+    def _(n):
+        for m in range(piece):
+            prepare(far_r + n * piece + m)
 
     def beside(above, here, below):
         cols = here.shape[0]
@@ -380,10 +431,10 @@
             + (low + high)
         )
 
-    def sweep(old, new, low, high, chunk, shift=0, cols=wide_cols):
-        @pl.loop(0, (high - low) // chunk)
-        def _(n):
-            i = low + n * chunk
+    def sweep(old, new, low, high, shift=0, cols=wide_cols):
+        chunk = max(m for m in range(1, MOST_ROWS + 1) if (high - low) % m == 0)
+
+        def work(i):
             lines = [old[i - 1 + m] for m in range(chunk + 2)]
             for m in range(chunk):
                 here = lines[m + 1]
@@ -392,10 +443,29 @@
                 )
                 new[i + m - shift] = fresh[:cols]
 
-    fields = (field_a, field_b)
+        if chunk == high - low:
+            work(low)
+        else:
+
+            @pl.loop(0, (high - low) // chunk)
+            def _(n):
+                work(low + n * chunk)
+
+    fields = (first,) + (field_b, field_a) * SWEEPS
+    smooth, other = fields[SWEEPS - 1], fields[SWEEPS]
     for turn in range(1, SWEEPS):
-        sweep(fields[(turn - 1) % 2], fields[turn % 2], 1, wide_rows - 1, 4)
-    smooth, other = fields[(SWEEPS - 1) % 2], fields[SWEEPS % 2]
+        sweep(fields[turn - 1], fields[turn], far_r + turn, wide_rows - far_r - turn)
+
+    def widen():
+        wait_halo(1)
+        for i in range(far_r):
+            prepare(i)
+            prepare(wide_rows - 1 - i)
+        for turn in range(1, SWEEPS):
+            sweep(fields[turn - 1], fields[turn], turn, far_r + turn)
+            sweep(
+                fields[turn - 1], fields[turn], wide_rows - far_r - turn, wide_rows - turn
+            )
 
     @pl.loop(0, coarse_rows)
     def _(a):
@@ -408,6 +478,8 @@
             total = left if total is None else total + left
         rows_sum[a] = total[:col_cells]
 
+    for copy in staged:
+        copy.wait()
     pairs = [
         rows_sum[a, pl.ds(0, coarse_cols, stride=2), :]
         + rows_sum[a, pl.ds(1, coarse_cols, stride=2), :]
@@ -422,7 +494,7 @@
 
     pl.semaphore_wait(ready, n_row - 1)
 
-    def exchange(send, recv, send_sem, recv_sem):
+    def exchange(send, recv, send_sem, recv_sem, meanwhile=None):
         def copy(d):
             target = lax.rem(me + d, devices)
             return pltpu.make_async_remote_copy(
@@ -439,6 +511,8 @@
             copy(d).start()
 
         recv[me] = send[me]
+        if meanwhile is not None:
+            meanwhile()
 
         @pl.loop(1, devices)
         def _(d):
@@ -446,7 +520,7 @@
 
         return copy
 
-    forward = exchange(send_a, recv_a, fwd_send, fwd_recv)
+    forward = exchange(send_a, recv_a, fwd_send, fwd_recv, widen)
 
     gathered = jnp.concatenate(
         [
@@ -499,20 +573,21 @@
         smooth[i] = smooth[i] + fine_corr[a]
         smooth[i + 1] = smooth[i + 1] + fine_corr[a]
 
-    fields = (smooth, other)
+    fields = (smooth, other) * SWEEPS
     for turn in range(SWEEPS):
         low, high = margin + 1 + turn, wide_rows - margin - 1 - turn
         if turn < SWEEPS - 1:
-            sweep(fields[turn % 2], fields[(turn + 1) % 2], low, high, 2)
+            sweep(fields[turn], fields[turn + 1], low, high)
         else:
-            sweep(fields[turn % 2], out, low, high, 2, low, col_cells)
-
-    for at in range(len(steps)):
-
-        @pl.when(exists(*steps[at]))
-        def _():
-            for n in range(2):
-                halo_copy(n, at).wait_send()
+            sweep(fields[turn], out, low, high, low, col_cells)
+
+    for far in range(2):
+        for step in portions[far]:
+
+            @pl.when(exists(*step))
+            def _():
+                for copy in halo_copies(far, *step):
+                    copy.wait_send()
 
     @pl.loop(1, devices)
     def _(d):
@@ -537,10 +612,10 @@
     return pl.pallas_call(
         body,
         out_shape=jax.ShapeDtypeStruct(source.shape, f32),
-        in_specs=[pl.BlockSpec(memory_space=pl.ANY)] * 2
-        + [pl.BlockSpec(memory_space=pltpu.VMEM)] * len(tables),
+        in_specs=[pl.BlockSpec(memory_space=pl.ANY)] * (2 + len(tables)),
         out_specs=pl.BlockSpec(memory_space=pltpu.VMEM),
-        scratch_shapes=[pltpu.VMEM(wide, f32)] * 6
+        scratch_shapes=[pltpu.VMEM(t.shape, f32) for t in tables]
+        + [pltpu.VMEM(wide, f32)] * 6
         + [
             pltpu.VMEM((coarse_rows, col_cells, z_cells), f32),
             pltpu.VMEM((blocks, 2 * col_cells, z_cells), f32),
@@ -549,8 +624,9 @@
             pltpu.VMEM((devices, 2 * kept, z_cells), f32),
             pltpu.VMEM((devices, 2 * kept, z_cells), f32),
             dma((2,)),
-            dma((2, 8)),
-            dma((2, 8)),
+            dma((len(tables),)),
+            dma((2, 2, 8)),
+            dma((2, 2, 8)),
             dma((devices,)),
             dma((devices,)),
             dma((devices,)),
@@ -574,6 +650,7 @@
         and blocks * (col_cells // 2) == z_cells
         and blocks == row_cells // 2 + SWEEPS
         and row_cells >= 2 * SWEEPS - 1
+        and (row_cells + 2 * SWEEPS) % (SUBLANES // 2) == 0
     )
 
 

time: 42.1 us -> 33.4 us (0.79)
  Pallas kernels: 40.3 us -> 31.6 us
    pallas_call x1, Pallas kernels: 40.3 us -> 31.6 us  [local_kernel(): pl.pallas_call(body, out_shape=jax.ShapeDtypeStruct(source.shape, f32), i...]
where the time goes in v2:
time: 33.4 us; the launch traced here: 33.2 us
  Pallas kernels  31.6 us (95%)
  local copies, waits for them, and re-layouts  1.62 us (5%)
    pallas_call x1, Pallas kernels, local_kernel(): pl.pallas_call(body, out_shape=jax.ShapeDtypeStruct(source.shape, f32), i...  31.6 us
    unnamed x1, local copies, waits for them, and re-layouts  1.62 us

profile of v2, /device:TPU:0, one launch (start us, length us, event | category | flops | bytes accessed | tf_op | source)
XLA Modules:
  0.0 33.2 jit_solution(15806499071316144244)
XLA Ops:
  0.0 31.6 %vstep.1 = f32[24,16,128]{2,1,0:T(8,128)} custom-call(f32[24,16,128]{2,1,0:T(8,128)} %refs_0_.1, f32[24,16,128]{2,1,0:T(8,128)} %refs_1_.1, f32[64,128]{1,0:T(8,128)} %constant.12.clone.refs_2_, f32[48,64]{1,0:T(8,128)} %constant.13.clone.refs_3_, f32[64,48]{1,0:T(8,128)} %constant.14.clone.refs_4_, f32[128,128]{1,0:T(8,128)} %constant.15.clone.refs_5_, ...), custom_call_target="tpu_custom_call" | custom-call | tf_op jit(solution)/shard_map/vstep/pallas_call | solution.py:612
  31.6 1.6 %copy.10 = f32[24,16,128]{2,1,0:T(8,128)} copy(f32[24,16,128]{2,1,0:T(8,128)} %vstep.1) | data formatting | bytes 393216

commit v3 on v2

--- a/solution.py
+++ b/solution.py
@@ -152,7 +152,7 @@
 
 MESH = pl.DeviceIdType.MESH
 SUBLANES = 8
-MOST_ROWS = 15
+MOST_ROWS = 40
 
 
 def plain_sine(length):
@@ -243,6 +243,7 @@
     field_b,
     rows_sum,
     fine_corr,
+    edge,
     send_a,
     recv_a,
     send_b,
@@ -251,6 +252,8 @@
     table_sem,
     halo_send,
     halo_recv,
+    edge_send,
+    edge_recv,
     fwd_send,
     fwd_recv,
     back_send,
@@ -320,19 +323,8 @@
     for copy in staged:
         copy.start()
 
-    near_r = SWEEPS
-    far_r = halo_r - near_r
-    portions = (steps, [step for step in steps if step[0]])
-
-    def landing(far, dr, dc):
-        if far:
-            rows = {-1: (0, far_r), 1: (halo_r + row_cells + near_r, far_r)}[dr]
-        else:
-            rows = {
-                -1: (far_r, near_r),
-                0: (halo_r, row_cells),
-                1: (halo_r + row_cells, near_r),
-            }[dr]
+    def landing(dr, dc):
+        rows = {-1: (0, halo_r), 0: (halo_r, row_cells), 1: (halo_r + row_cells, halo_r)}[dr]
         cols = {
             -1: (col_cells + halo_c, halo_c),
             0: (0, col_cells),
@@ -340,64 +332,52 @@
         }[dc]
         return pl.ds(*rows), pl.ds(*cols)
 
-    def leaving(far, dr, dc):
-        if far:
-            rows = {-1: (near_r, far_r), 1: (row_cells - halo_r, far_r)}[dr]
-        else:
-            rows = {-1: (0, near_r), 0: (0, row_cells), 1: (row_cells - near_r, near_r)}[dr]
+    def leaving(dr, dc):
+        rows = {-1: (0, halo_r), 0: (0, row_cells), 1: (row_cells - halo_r, halo_r)}[dr]
         cols = {-1: (0, halo_c), 0: (0, col_cells), 1: (col_cells - halo_c, halo_c)}[dc]
         return pl.ds(*rows), pl.ds(*cols)
 
-    def halo_copies(far, dr, dc):
+    def halo_copies(dr, dc):
         at = steps.index((dr, dc))
         return [
             pltpu.make_async_remote_copy(
-                src_ref=here.at[leaving(far, dr, dc)],
-                dst_ref=wide.at[landing(far, -dr, -dc)],
-                send_sem=halo_send.at[far, n, at],
-                recv_sem=halo_recv.at[far, n, at],
+                src_ref=here.at[leaving(dr, dc)],
+                dst_ref=wide.at[landing(-dr, -dc)],
+                send_sem=halo_send.at[n, at],
+                recv_sem=halo_recv.at[n, at],
                 device_id=(my_row + dr, my_col + dc),
                 device_id_type=MESH,
             )
             for n, (here, wide) in enumerate(arrays)
         ]
 
-    def start_halo(far):
-        for step in portions[far]:
-
-            @pl.when(exists(*step))
-            def _():
-                for copy in halo_copies(far, *step):
-                    copy.start()
-
-    def fill_halo(far):
-        for step in portions[far]:
-
-            @pl.when(jnp.logical_not(exists(*step)))
-            def _():
-                rows, cols = landing(far, *step)
-                for _, wide in arrays:
-                    wide[rows, cols] = jnp.zeros((rows.size, cols.size, z_cells), jnp.float32)
-
-    def wait_halo(far):
-        for dr, dc in portions[far]:
-            @pl.when(exists(-dr, -dc))
-            def _():
-                for copy in halo_copies(far, dr, dc):
-                    copy.wait_recv()
-
     pl.semaphore_wait(barrier, greeted)
-    start_halo(0)
+    for step in steps:
+
+        @pl.when(exists(*step))
+        def _():
+            for copy in halo_copies(*step):
+                copy.start()
+
     for d in range(1, n_row):
         pl.semaphore_signal(
             ready, 1, device_id=(lax.rem(my_row + d, n_row), my_col), device_id_type=MESH
         )
-    start_halo(1)
-    fill_halo(0)
-    fill_halo(1)
+    for step in steps:
+
+        @pl.when(jnp.logical_not(exists(*step)))
+        def _():
+            rows, cols = landing(*step)
+            for _, wide in arrays:
+                wide[rows, cols] = jnp.zeros((rows.size, cols.size, z_cells), jnp.float32)
+
     for copy in own:
         copy.wait()
-    wait_halo(0)
+    for dr, dc in steps:
+        @pl.when(exists(-dr, -dc))
+        def _():
+            for copy in halo_copies(dr, dc):
+                copy.wait_recv()
 
     wide_rows = wide_s.shape[0]
     col_at = lax.broadcasted_iota(jnp.int32, (wide_cols, z_cells), 0)
@@ -416,10 +396,10 @@
 
     piece = SUBLANES // 2
 
-    @pl.loop(0, (row_cells + 2 * near_r) // piece)
+    @pl.loop(0, wide_rows // piece)
     def _(n):
         for m in range(piece):
-            prepare(far_r + n * piece + m)
+            prepare(n * piece + m)
 
     def beside(above, here, below):
         cols = here.shape[0]
@@ -454,18 +434,29 @@
     fields = (first,) + (field_b, field_a) * SWEEPS
     smooth, other = fields[SWEEPS - 1], fields[SWEEPS]
     for turn in range(1, SWEEPS):
-        sweep(fields[turn - 1], fields[turn], far_r + turn, wide_rows - far_r - turn)
-
-    def widen():
-        wait_halo(1)
-        for i in range(far_r):
-            prepare(i)
-            prepare(wide_rows - 1 - i)
-        for turn in range(1, SWEEPS):
-            sweep(fields[turn - 1], fields[turn], turn, far_r + turn)
-            sweep(
-                fields[turn - 1], fields[turn], wide_rows - far_r - turn, wide_rows - turn
-            )
+        sweep(fields[turn - 1], fields[turn], turn, wide_rows - turn)
+
+    edge_rows = halo_r - 1
+    edge_at = (0, halo_r + row_cells + 1)
+
+    def edge_copy(dr):
+        return pltpu.make_async_remote_copy(
+            src_ref=smooth.at[
+                pl.ds(halo_r + (1 if dr < 0 else row_cells - halo_r), edge_rows)
+            ],
+            dst_ref=edge.at[1 if dr < 0 else 0],
+            send_sem=edge_send.at[1 if dr < 0 else 0],
+            recv_sem=edge_recv.at[1 if dr < 0 else 0],
+            device_id=(my_row + dr, my_col),
+            device_id_type=MESH,
+        )
+
+    def start_edges():
+        for dr in (-1, 1):
+
+            @pl.when(exists(dr, 0))
+            def _():
+                edge_copy(dr).start()
 
     @pl.loop(0, coarse_rows)
     def _(a):
@@ -520,7 +511,7 @@
 
         return copy
 
-    forward = exchange(send_a, recv_a, fwd_send, fwd_recv, widen)
+    forward = exchange(send_a, recv_a, fwd_send, fwd_recv, start_edges)
 
     gathered = jnp.concatenate(
         [
@@ -565,6 +556,22 @@
                     a * coarse_cols : (a + 1) * coarse_cols
                 ]
 
+    for dr in (-1, 1):
+        slot = 1 if dr < 0 else 0
+
+        @pl.when(exists(dr, 0))
+        def _():
+            edge_copy(dr).wait_send()
+
+        @pl.when(exists(-dr, 0))
+        def _():
+            edge_copy(dr).wait_recv()
+            smooth[pl.ds(edge_at[slot], edge_rows)] = edge[slot]
+
+        @pl.when(jnp.logical_not(exists(-dr, 0)))
+        def _():
+            smooth[pl.ds(edge_at[slot], edge_rows)] = jnp.zeros(edge.shape[1:], jnp.float32)
+
     margin = halo_r - (blocks - coarse_rows)
 
     @pl.loop(0, blocks)
@@ -581,13 +588,12 @@
         else:
             sweep(fields[turn], out, low, high, low, col_cells)
 
-    for far in range(2):
-        for step in portions[far]:
-
-            @pl.when(exists(*step))
-            def _():
-                for copy in halo_copies(far, *step):
-                    copy.wait_send()
+    for step in steps:
+
+        @pl.when(exists(*step))
+        def _():
+            for copy in halo_copies(*step):
+                copy.wait_send()
 
     @pl.loop(1, devices)
     def _(d):
@@ -602,7 +608,7 @@
     kept = coarse_z // devices
     blocks = n_col * kept
     tables = solve_tables(n_row, n_col, kept, coarse_rows, coarse_cols, coarse_z)
-    wide = (row_cells + 2 * (2 * SWEEPS - 1), col_cells + 2 * SUBLANES, z_cells)
+    wide = (row_cells + 2 * SWEEPS, col_cells + 2 * SUBLANES, z_cells)
     dma = pltpu.SemaphoreType.DMA
     f32 = jnp.float32
 
@@ -619,14 +625,17 @@
         + [
             pltpu.VMEM((coarse_rows, col_cells, z_cells), f32),
             pltpu.VMEM((blocks, 2 * col_cells, z_cells), f32),
+            pltpu.VMEM((2, SWEEPS - 1) + wide[1:], f32),
             pltpu.VMEM((devices, kept, z_cells), f32),
             pltpu.VMEM((devices, kept, z_cells), f32),
             pltpu.VMEM((devices, 2 * kept, z_cells), f32),
             pltpu.VMEM((devices, 2 * kept, z_cells), f32),
             dma((2,)),
             dma((len(tables),)),
-            dma((2, 2, 8)),
-            dma((2, 2, 8)),
+            dma((2, 8)),
+            dma((2, 8)),
+            dma((2,)),
+            dma((2,)),
             dma((devices,)),
             dma((devices,)),
             dma((devices,)),
@@ -649,7 +658,7 @@
         and col_cells == 2 * SUBLANES
         and blocks * (col_cells // 2) == z_cells
         and blocks == row_cells // 2 + SWEEPS
-        and row_cells >= 2 * SWEEPS - 1
+        and row_cells >= 2 * SWEEPS
         and (row_cells + 2 * SWEEPS) % (SUBLANES // 2) == 0
     )
 

time: 33.4 us -> 31.2 us (0.934)
  Pallas kernels: 31.6 us -> 29.4 us
    pallas_call x1, Pallas kernels: 31.6 us -> 29.4 us  [local_kernel(): pl.pallas_call(body, out_shape=jax.ShapeDtypeStruct(source.shape, f32), i...]
where the time goes in v3:
time: 31.2 us; the launch traced here: 31.1 us
  Pallas kernels  29.4 us (94%)
  local copies, waits for them, and re-layouts  1.62 us (5%)
    pallas_call x1, Pallas kernels, local_kernel(): pl.pallas_call(body, out_shape=jax.ShapeDtypeStruct(source.shape, f32), i...  29.4 us
    unnamed x1, local copies, waits for them, and re-layouts  1.62 us

profile of v3, /device:TPU:0, one launch (start us, length us, event | category | flops | bytes accessed | tf_op | source)
XLA Modules:
  0.0 31.1 jit_solution(13608610684589523791)
XLA Ops:
  0.0 29.4 %vstep.1 = f32[24,16,128]{2,1,0:T(8,128)} custom-call(f32[24,16,128]{2,1,0:T(8,128)} %refs_0_.1, f32[24,16,128]{2,1,0:T(8,128)} %refs_1_.1, f32[64,128]{1,0:T(8,128)} %constant.12.clone.refs_2_, f32[48,64]{1,0:T(8,128)} %constant.13.clone.refs_3_, f32[64,48]{1,0:T(8,128)} %constant.14.clone.refs_4_, f32[128,128]{1,0:T(8,128)} %constant.15.clone.refs_5_, ...), custom_call_target="tpu_custom_call" | custom-call | tf_op jit(solution)/shard_map/vstep/pallas_call | solution.py:618
  29.5 1.6 %copy.10 = f32[24,16,128]{2,1,0:T(8,128)} copy(f32[24,16,128]{2,1,0:T(8,128)} %vstep.1) | data formatting | bytes 393216

commit v4 on v3

--- a/solution.py
+++ b/solution.py
@@ -212,10 +212,16 @@
     return x
 
 
-def exact_dot(a, b, contract):
-    return lax.dot_general(
-        a, b, (contract, ((), ())), precision=HIGHEST, preferred_element_type=jnp.float32
-    )
+def split_dot(a, b, contract):
+    def parts(x):
+        high = x.astype(jnp.bfloat16)
+        return high, (x - high.astype(jnp.float32)).astype(jnp.bfloat16)
+
+    def product(x, y):
+        return lax.dot_general(x, y, (contract, ((), ())), preferred_element_type=jnp.float32)
+
+    (a_high, a_low), (b_high, b_low) = parts(a), parts(b)
+    return product(a_high, b_high) + (product(a_high, b_low) + product(a_low, b_high))
 
 
 def step_kernel(
@@ -477,7 +483,7 @@
         for a in range(coarse_rows)
     ]
     blank = jnp.zeros(((blocks - coarse_rows) * coarse_cols, z_cells), jnp.float32)
-    along_z = exact_dot(
+    along_z = split_dot(
         table_z[...], jnp.concatenate(pairs + [blank], axis=0), ((1,), (1,))
     )
     for q in range(devices):
@@ -497,7 +503,7 @@
                 device_id_type=MESH,
             )
 
-        @pl.loop(1, devices)
+        @pl.loop(1, devices, unroll=True)
         def _(d):
             copy(d).start()
 
@@ -522,11 +528,11 @@
         ],
         axis=0,
     )
-    along_r = exact_dot(forward_r[...], gathered, ((1,), (0,)))
-    spectrum = exact_dot(along_r, table_c[...], ((1,), (0,)))
+    along_r = split_dot(forward_r[...], gathered, ((1,), (0,)))
+    spectrum = split_dot(along_r, table_c[...], ((1,), (0,)))
     scaled = spectrum / (base[...] + lam_z[me])
-    back_c = exact_dot(scaled, table_c[...], ((1,), (1,)))
-    back_r = exact_dot(window_r[...], back_c, ((1,), (0,)))
+    back_c = split_dot(scaled, table_c[...], ((1,), (1,)))
+    back_r = split_dot(window_r[...], back_c, ((1,), (0,)))
     lane = lax.broadcasted_iota(jnp.int32, (blocks, z_cells), 1)
     column = lane // (kept * coarse_cols)
     late = lane % coarse_cols >= coarse_cols // 2
@@ -549,7 +555,7 @@
     modes = devices * kept
     for part in range(2):
         lines = recv_b[:, pl.ds(part * kept, kept)].reshape(modes, z_cells)
-        values = exact_dot(jnp.transpose(lines), table_z[...], ((1,), (0,)))
+        values = split_dot(jnp.transpose(lines), table_z[...], ((1,), (0,)))
         for a in range(blocks):
             for odd in range(2):
                 fine_corr[a, pl.ds(part * col_cells + odd, coarse_cols, stride=2), :] = values[

time: 31.2 us -> 30.7 us (0.984)
  Pallas kernels: 29.4 us -> 28.9 us
    pallas_call x1, Pallas kernels: 29.4 us -> 28.9 us  [local_kernel(): pl.pallas_call(body, out_shape=jax.ShapeDtypeStruct(source.shape, f32), i...]
where the time goes in v4:
time: 30.7 us; the launch traced here: 30.5 us
  Pallas kernels  28.9 us (94%)
  local copies, waits for them, and re-layouts  1.62 us (5%)
    pallas_call x1, Pallas kernels, local_kernel(): pl.pallas_call(body, out_shape=jax.ShapeDtypeStruct(source.shape, f32), i...  28.9 us
    unnamed x1, local copies, waits for them, and re-layouts  1.62 us

profile of v4, /device:TPU:0, one launch (start us, length us, event | category | flops | bytes accessed | tf_op | source)
XLA Modules:
  0.0 30.5 jit_solution(6708640769462453830)
XLA Ops:
  0.0 28.9 %vstep.1 = f32[24,16,128]{2,1,0:T(8,128)} custom-call(f32[24,16,128]{2,1,0:T(8,128)} %refs_0_.1, f32[24,16,128]{2,1,0:T(8,128)} %refs_1_.1, f32[64,128]{1,0:T(8,128)} %constant.12.clone.refs_2_, f32[48,64]{1,0:T(8,128)} %constant.13.clone.refs_3_, f32[64,48]{1,0:T(8,128)} %constant.14.clone.refs_4_, f32[128,128]{1,0:T(8,128)} %constant.15.clone.refs_5_, ...), custom_call_target="tpu_custom_call" | custom-call | tf_op jit(solution)/shard_map/vstep/pallas_call | solution.py:624
  28.9 1.6 %copy.10 = f32[24,16,128]{2,1,0:T(8,128)} copy(f32[24,16,128]{2,1,0:T(8,128)} %vstep.1) | data formatting | bytes 393216

commit v5 on v4

--- a/solution.py
+++ b/solution.py
@@ -511,13 +511,15 @@
         if meanwhile is not None:
             meanwhile()
 
-        @pl.loop(1, devices)
+        @pl.loop(1, devices, unroll=True)
+        def _(d):
+            copy(d).wait_send()
+
+        @pl.loop(1, devices, unroll=True)
         def _(d):
             copy(d).wait_recv()
 
-        return copy
-
-    forward = exchange(send_a, recv_a, fwd_send, fwd_recv, start_edges)
+    exchange(send_a, recv_a, fwd_send, fwd_recv, start_edges)
 
     gathered = jnp.concatenate(
         [
@@ -550,7 +552,15 @@
             jnp.where(late, left, right), coarse_cols
         ).reshape(n_col, kept, z_cells)
 
-    backward = exchange(send_b, recv_b, back_send, back_recv)
+    def end_halo():
+        for step in steps:
+
+            @pl.when(exists(*step))
+            def _():
+                for copy in halo_copies(*step):
+                    copy.wait_send()
+
+    exchange(send_b, recv_b, back_send, back_recv, end_halo)
 
     modes = devices * kept
     for part in range(2):
@@ -593,18 +603,6 @@
             sweep(fields[turn], fields[turn + 1], low, high)
         else:
             sweep(fields[turn], out, low, high, low, col_cells)
-
-    for step in steps:
-
-        @pl.when(exists(*step))
-        def _():
-            for copy in halo_copies(*step):
-                copy.wait_send()
-
-    @pl.loop(1, devices)
-    def _(d):
-        forward(d).wait_send()
-        backward(d).wait_send()
 
 
 def local_kernel(n_row, n_col, source, coefficient):

time: 30.7 us -> 30.4 us (level)
  no operation moved by 1% of the time
where the time goes in v5:
time: 30.4 us; the launch traced here: 30.2 us
  Pallas kernels  28.6 us (94%)
  local copies, waits for them, and re-layouts  1.62 us (5%)
    pallas_call x1, Pallas kernels, local_kernel(): pl.pallas_call(body, out_shape=jax.ShapeDtypeStruct(source.shape, f32), i...  28.6 us
    unnamed x1, local copies, waits for them, and re-layouts  1.62 us

profile of v5, /device:TPU:0, one launch (start us, length us, event | category | flops | bytes accessed | tf_op | source)
XLA Modules:
  0.0 30.2 jit_solution(8495582959153458390)
XLA Ops:
  0.0 28.6 %vstep.1 = f32[24,16,128]{2,1,0:T(8,128)} custom-call(f32[24,16,128]{2,1,0:T(8,128)} %refs_0_.1, f32[24,16,128]{2,1,0:T(8,128)} %refs_1_.1, f32[64,128]{1,0:T(8,128)} %constant.12.clone.refs_2_, f32[48,64]{1,0:T(8,128)} %constant.13.clone.refs_3_, f32[64,48]{1,0:T(8,128)} %constant.14.clone.refs_4_, f32[128,128]{1,0:T(8,128)} %constant.15.clone.refs_5_, ...), custom_call_target="tpu_custom_call" | custom-call | tf_op jit(solution)/shard_map/vstep/pallas_call | solution.py:622
  28.6 1.6 %copy.10 = f32[24,16,128]{2,1,0:T(8,128)} copy(f32[24,16,128]{2,1,0:T(8,128)} %vstep.1) | data formatting | bytes 393216
